TPU v7x, 128 devices: a whole 4x4x4 slice. The times are simulated.
128 devices in a mesh: wide: 32 (over y, z_lo, x), narrow: 4 (over z_hi, core).
Axes of the slice: x: 4, y: 4, z: 4 (z_hi: 2, z_lo: 2; z = z_hi * 2 + z_lo), core: 2. Of those that a mesh axis runs over, the one named last changes fastest.
Arguments:
- loads: float32 [98304, 512], P('wide', 'narrow'), may hold values from -6 to 6
- start: float32 [98304, 512], P('wide', 'narrow'), may hold values from -6 to 6
- stiffness: bfloat16 [128, 1024, 1024], P('wide')
- local_inverse: bfloat16 [128, 1024, 1024], P('wide')
- modes: bfloat16 [128, 1024, 32], P('wide'), may hold values from -0.1875 to 0.1875
- coarse_inverse: float32 [4096, 4096], P('wide', 'narrow'), as said below
- margin_rows: int32 [128, 256], P('wide'), may hold values from 0 to 98303, as said below
Outputs:
- displacement: float32 [98304, 512], P('wide', 'narrow')
- final_residual: float32 [98304, 512], P('wide', 'narrow')
Inputs may be any that keep to these rules, and one draw needn't show every extreme that they name: Row s lists 256 distinct rows of loads, none of them rows s * 768 to s * 768 + 767. Call rows i * 4 * 768 to (i + 1) * 4 * 768 - 1 block i. For every i, the entries of rows i * 4 to (i + 1) * 4 - 1 of margin_rows fall at most 48 times into any one block, and exactly 48 times into some block. coarse_inverse equals its transpose.
All inputs are finite; a program needn't handle non-finite values.
Results may differ from a plain program's by a relative error of at most 0.0062.
Values may be sent and summed in bfloat16 or wider, within the bound.
A program may use at most 128 MiB of HBM per device.

v0:
```python
import jax
import jax.numpy as jnp
from jax import lax
from jax.sharding import PartitionSpec as P

ITERS = 2
damping = 0.5


def apply_each(matrices, vectors):
    return jnp.einsum("sij,sjc->sic", matrices, vectors, preferred_element_type=jnp.float32)


def shards(loads, start, stiffness, local_inverse, modes, coarse_inverse, margin_rows):
    owners = lax.axis_size("wide")
    sub_count, margin_count = margin_rows.shape
    matrix_order = stiffness.shape[1]
    core_count = matrix_order - margin_count
    held_rows, col_count = loads.shape
    mode_count = modes.shape[2]
    coarse_rows_dev = sub_count * mode_count
    capacity = 3 * sub_count * margin_count // (2 * owners)
    flat_rows = margin_rows.reshape(-1)
    source = flat_rows // held_rows
    remote_row = flat_rows - source * held_rows
    onehot = (source[:, None] == jnp.arange(owners, dtype=jnp.int32)[None, :]).astype(jnp.int32)
    before = jnp.cumsum(onehot, axis=0) - onehot
    placed = source * capacity + jnp.sum(before * onehot, axis=1)
    requested = jnp.full((owners * capacity,), -1, jnp.int32).at[placed].set(remote_row)
    wanted = lax.all_to_all(
        requested.reshape(owners, capacity), "wide", split_axis=0, concat_axis=0, tiled=True
    )
    usable = (wanted >= 0).reshape(-1)
    picked = jnp.where(usable, wanted.reshape(-1), 0)

    def gather_local(field):
        field_low = field.astype(jnp.bfloat16)
        outgoing = jnp.where(usable[:, None], field_low[picked], jnp.zeros((), jnp.bfloat16))
        incoming = lax.all_to_all(
            outgoing.reshape(owners, capacity, col_count),
            "wide",
            split_axis=0,
            concat_axis=0,
            tiled=True,
        )
        outer_part = incoming.reshape(owners * capacity, col_count)[placed].reshape(
            sub_count, margin_count, col_count
        )
        core_part = field_low.reshape(sub_count, core_count, col_count)
        return jnp.concatenate([core_part, outer_part], axis=1)

    def assemble_parts(parts):
        outer_part = parts[:, core_count:, :].reshape(sub_count * margin_count, col_count)
        outgoing = jnp.zeros((owners * capacity, col_count), jnp.float32).at[placed].set(outer_part)
        incoming = lax.all_to_all(
            outgoing.reshape(owners, capacity, col_count),
            "wide",
            split_axis=0,
            concat_axis=0,
            tiled=True,
        )
        summed = parts[:, :core_count, :].reshape(held_rows, col_count)
        return summed.at[picked].add(incoming.reshape(owners * capacity, col_count))

    def residual_of(field):
        return loads - assemble_parts(apply_each(stiffness, gather_local(field)))

    field = start
    for iteration in range(ITERS):
        residual = residual_of(field)
        restricted = gather_local(residual)
        solved_local = apply_each(local_inverse, restricted)
        projection = jnp.einsum(
            "sim,sic->smc", modes, restricted, preferred_element_type=jnp.float32
        )
        solve_projection = projection.reshape(coarse_rows_dev, col_count)
        gathered = lax.all_gather(solve_projection, "wide", axis=0, tiled=True)
        tile_width = coarse_inverse.shape[1]
        row_offset = lax.axis_index("narrow") * tile_width
        selected = lax.dynamic_slice_in_dim(
            lax.all_gather(gathered, "narrow", axis=1, tiled=True), row_offset, tile_width, 0
        )
        partial_sums = jnp.dot(coarse_inverse, selected, precision=lax.Precision.HIGHEST)
        coarse = lax.psum_scatter(partial_sums, "narrow", scatter_dimension=1, tiled=True)
        lifted = jnp.einsum(
            "sim,smc->sic",
            modes.astype(jnp.float32),
            coarse.reshape(sub_count, mode_count, col_count),
            precision=lax.Precision.HIGHEST,
        )
        change = assemble_parts(damping * solved_local + lifted)
        field = field + change
    return (field, residual_of(field))


def solution(mesh):
    placed = (
        P("wide", "narrow"),
        P("wide", "narrow"),
        P("wide", None, None),
        P("wide", None, None),
        P("wide", None, None),
        P("wide", "narrow"),
        P("wide", None),
    )
    return jax.shard_map(
        shards,
        mesh=mesh,
        in_specs=placed,
        out_specs=(P("wide", "narrow"), P("wide", "narrow")),
        check_vma=False,
    )
```

profile of v0, /device:TPU:0, one launch (start us, length us, event | category | flops | bytes accessed | tf_op | source)
XLA Modules:
  0.0 880.2 jit_solution(7259748184903397401)
XLA Ops:
  10.8 9.0 %reduce-window.6 = s32[32,8,128]{2,1,0:T(8,128)S(1)} reduce-window(s32[32,8,128]{2,1,0:T(8,128)S(1)} %fusion.34, s32[]{:T(128)} %constant.15.clone.1), window={size=1x1x128 pad=0_0x0_0x127_0}, to_apply=%region_0.1 | reduce-window | flops 4161536 | bytes 262148 | tf_op jit(solution)/shard_map/reduce-window
  25.4 8.8 all-to-all-start
  52.2 9.4 %all-to-all-done.1 = bf16[32,48,128]{2,1,0:T(8,128)(2,1)S(1)} async-done(((bf16[32,48,128]{2,1,0:T(8,128)(2,1)}), bf16[32,48,128]{2,1,0:T(8,128)(2,1)S(1)}, u32[]{:S(2)}, u32[]{:S(2)}) %all-to-all-start.1) | async-done | bytes 393248 | tf_op jit(solution)/shard_map/all_to_all | solution.py:39
  84.6 8.8 %all-to-all-done.2 = f32[32,48,128]{2,1,0:T(8,128)S(1)} async-done(((f32[32,48,128]{2,1,0:T(8,128)}), f32[32,48,128]{2,1,0:T(8,128)S(1)}, u32[]{:S(2)}, u32[]{:S(2)}) %all-to-all-start.2) | async-done | bytes 786464 | tf_op jit(solution)/shard_map/all_to_all | solution.py:55
  93.4 9.5 %scatter_fusion = f32[3072,128]{1,0:T(8,128)S(1)} fusion(f32[3072,128]{1,0:T(8,128)S(1)} %bitcast.119, s32[1536]{0:T(1024)S(1)} %fusion.35, f32[1536,128]{1,0:T(8,128)S(1)} %bitcast.132), kind=kCustom, calls=%fused_computation.12 | custom fusion | flops 196608 | bytes 2365440 | tf_op jit(solution)/shard_map/scatter-add | solution.py:63
  113.6 9.2 %all-to-all-done.3 = bf16[32,48,128]{2,1,0:T(8,128)(2,1)S(1)} async-done(((bf16[32,48,128]{2,1,0:T(8,128)(2,1)}), bf16[32,48,128]{2,1,0:T(8,128)(2,1)S(1)}, u32[]{:S(2)}, u32[]{:S(2)}) %all-to-all-start.3) | async-done | bytes 393248 | tf_op jit(solution)/shard_map/all_to_all | solution.py:39
  127.3 151.5 %all-gather.5.cloned.1.call-done = f32[4096,128]{1,0:T(8,128)} async-done(((f32[128,128]{1,0:T(8,128)}), f32[4096,128]{1,0:T(8,128)}) %all-gather.5.cloned.1.call-update) | async-done | bytes 2097168 | tf_op jit(solution)/shard_map/all_gather | solution.py:77
  278.9 65.2 %all-gather.7.cloned.1.call-done = f32[4096,512]{1,0:T(8,128)} async-done(((f32[4096,128]{1,0:T(8,128)}), f32[4096,512]{1,0:T(8,128)}) %all-gather.7.cloned.1.call-update) | async-done | bytes 8388624 | tf_op jit(solution)/shard_map/all_gather | solution.py:81
  349.8 26.5 %reduce-scatter.3.cloned.1.call-done = f32[128,128]{0,1:T(8,128)} async-done(((f32[128,512]{0,1:T(8,128)}), f32[128,128]{0,1:T(8,128)}) %reduce-scatter.3.cloned.1.call-update) | async-done | bytes 65552 | tf_op jit(solution)/shard_map/reduce_scatter | solution.py:84
  390.7 7.2 all-to-all-start.4
  399.9 12.1 %all-to-all-done.4 = f32[32,48,128]{2,1,0:T(8,128)S(1)} async-done(((f32[32,48,128]{2,1,0:T(8,128)}), f32[32,48,128]{2,1,0:T(8,128)S(1)}, u32[]{:S(2)}, u32[]{:S(2)}) %all-to-all-start.4) | async-done | bytes 786464 | tf_op jit(solution)/shard_map/all_to_all | solution.py:55
  412.0 9.7 %scatter_fusion.1 = f32[3072,128]{1,0:T(8,128)S(1)} fusion(f32[3072,128]{1,0:T(8,128)S(1)} %bitcast_add_fusion.1, s32[1536]{0:T(1024)S(1)} %fusion.35, f32[1536,128]{1,0:T(8,128)S(1)} %bitcast.135), kind=kCustom, calls=%fused_computation.14 | custom fusion | flops 196608 | bytes 2365440 | tf_op jit(solution)/shard_map/scatter-add | solution.py:63
  432.3 8.5 all-to-all-done.5
  474.2 10.8 %scatter_fusion.2 = f32[3072,128]{1,0:T(8,128)} fusion(f32[3072,128]{1,0:T(8,128)} %bitcast.120, s32[1536]{0:T(1024)S(1)} %fusion.35, f32[1536,128]{1,0:T(8,128)S(1)} %bitcast.133), kind=kCustom, calls=%fused_computation.16 | custom fusion | flops 196608 | bytes 2365440 | tf_op jit(solution)/shard_map/scatter-add | solution.py:63
  497.7 8.5 all-to-all-done.7
  513.1 149.8 %all-gather.9.cloned.1.call-done = f32[4096,128]{1,0:T(8,128)} async-done(((f32[128,128]{1,0:T(8,128)}), f32[4096,128]{1,0:T(8,128)}) %all-gather.9.cloned.1.call-update) | async-done | bytes 2097168 | tf_op jit(solution)/shard_map/all_gather | solution.py:77
  663.4 64.8 %all-gather.11.cloned.1.call-done = f32[4096,512]{1,0:T(8,128)} async-done(((f32[4096,128]{1,0:T(8,128)}), f32[4096,512]{1,0:T(8,128)}) %all-gather.11.cloned.1.call-update) | async-done | bytes 8388624 | tf_op jit(solution)/shard_map/all_gather | solution.py:81
  733.8 26.4 %reduce-scatter.5.cloned.1.call-done = f32[128,128]{0,1:T(8,128)} async-done(((f32[128,512]{0,1:T(8,128)}), f32[128,128]{0,1:T(8,128)}) %reduce-scatter.5.cloned.1.call-update) | async-done | bytes 65552 | tf_op jit(solution)/shard_map/reduce_scatter | solution.py:84
  777.2 7.2 all-to-all-start.8
  787.1 11.5 %all-to-all-done.8 = f32[32,48,128]{2,1,0:T(8,128)S(1)} async-done(((f32[32,48,128]{2,1,0:T(8,128)}), f32[32,48,128]{2,1,0:T(8,128)S(1)}, u32[]{:S(2)}, u32[]{:S(2)}) %all-to-all-start.8) | async-done | bytes 786464 | tf_op jit(solution)/shard_map/all_to_all | solution.py:55
  798.6 10.8 %scatter_fusion.3 = f32[3072,128]{1,0:T(8,128)} fusion(f32[3072,128]{1,0:T(8,128)} %bitcast_add_fusion, s32[1536]{0:T(1024)S(1)} %fusion.35, f32[1536,128]{1,0:T(8,128)S(1)} %bitcast.134), kind=kCustom, calls=%fused_computation.18 | custom fusion | flops 196608 | bytes 2365440 | tf_op jit(solution)/shard_map/scatter-add | solution.py:63
  820.1 9.4 %all-to-all-done.9 = bf16[32,48,128]{2,1,0:T(8,128)(2,1)S(1)} async-done(((bf16[32,48,128]{2,1,0:T(8,128)(2,1)}), bf16[32,48,128]{2,1,0:T(8,128)(2,1)S(1)}, u32[]{:S(2)}, u32[]{:S(2)}) %all-to-all-start.9) | async-done | bytes 393248 | tf_op jit(solution)/shard_map/all_to_all | solution.py:39
  852.6 8.5 all-to-all-done.10
  861.0 9.5 %scatter_fusion.4 = f32[3072,128]{1,0:T(8,128)S(1)} fusion(f32[3072,128]{1,0:T(8,128)S(1)} %bitcast.118, s32[1536]{0:T(1024)S(1)} %fusion.35, f32[1536,128]{1,0:T(8,128)S(1)} %bitcast.131), kind=kCustom, calls=%fused_computation.20 | custom fusion | flops 196608 | bytes 2365440 | tf_op jit(solution)/shard_map/scatter-add | solution.py:63
  (144 shorter events, 212.9 us)
Async XLA Ops:
  7.2 336.9 %copy-start = (f32[128,1024]{1,0:T(8,128)S(1)}, f32[128,1024]{1,0:T(8,128)}, u32[]{:S(2)}) copy-start(f32[128,1024]{1,0:T(8,128)} %param.12) | copy-start | bytes 1572868
  20.3 52.7 %copy-start.10 = (s32[1024,1]{0,1:T(1,128)}, s32[1024,1]{0,1:T(1,128)S(1)}, u32[]{:S(2)}) copy-start(s32[1024,1]{0,1:T(1,128)S(1)} %compare_select_fusion.2) | copy-start | bytes 12292
  25.4 17.0 %all-to-all-start = ((s32[32,1,48]{2,1,0:T(1,128)}), s32[32,1,48]{2,1,0:T(1,128)S(1)}, u32[]{:S(2)}, u32[]{:S(2)}) async-start(s32[32,1,48]{2,1,0:T(1,128)} %all_to_all.38), calls=%async_computation | async-start | bytes 32768 | tf_op jit(solution)/shard_map/all_to_all | solution.py:30
  42.4 65.3 %copy-start.5 = (pred[32,48]{1,0:T(8,128)(4,1)}, pred[32,48]{1,0:T(8,128)(4,1)S(1)}, u32[]{:S(2)}) copy-start(pred[32,48]{1,0:T(8,128)(4,1)S(1)} %compare_bitcast_fusion) | copy-start | bytes 4612
  48.0 13.6 %all-to-all-start.1 = ((bf16[32,48,128]{2,1,0:T(8,128)(2,1)}), bf16[32,48,128]{2,1,0:T(8,128)(2,1)S(1)}, u32[]{:S(2)}, u32[]{:S(2)}) async-start(bf16[32,48,128]{2,1,0:T(8,128)(2,1)} %broadcast_select_fusion.4), calls=%async_computation.1 | async-start | bytes 786432 | tf_op jit(solution)/shard_map/all_to_all | solution.py:39
  52.1 19.8 %copy-start.7 = (s32[1024]{0:T(1024)}, s32[1024]{0:T(1024)S(1)}, u32[]{:S(2)}) copy-start(s32[1024]{0:T(1024)S(1)} %broadcast_clamp_fusion) | copy-start | bytes 12292
  77.4 16.0 %all-to-all-start.2 = ((f32[32,48,128]{2,1,0:T(8,128)}), f32[32,48,128]{2,1,0:T(8,128)S(1)}, u32[]{:S(2)}, u32[]{:S(2)}) async-start(f32[32,48,128]{2,1,0:T(8,128)} %bitcast.137), calls=%async_computation.2 | async-start | bytes 1572864 | tf_op jit(solution)/shard_map/all_to_all | solution.py:55
  107.6 15.2 %copy-start.8 = (s32[1024]{0:T(1024)S(1)}, s32[1024]{0:T(1024)}, u32[]{:S(2)}) copy-start(s32[1024]{0:T(1024)} %copy-done.7) | copy-start | bytes 12292
  108.7 14.1 %all-to-all-start.3 = ((bf16[32,48,128]{2,1,0:T(8,128)(2,1)}), bf16[32,48,128]{2,1,0:T(8,128)(2,1)S(1)}, u32[]{:S(2)}, u32[]{:S(2)}) async-start(bf16[32,48,128]{2,1,0:T(8,128)(2,1)} %broadcast_select_fusion.3), calls=%async_computation.3 | async-start | bytes 786432 | tf_op jit(solution)/shard_map/all_to_all | solution.py:39
  113.1 165.7 %all-gather.5.cloned.1.call-start = ((), (), s32[]{:S(2)}) async-start(), calls=%async_computation.13 | async-start | bytes 2162688 | tf_op jit(solution)/shard_map/all_gather | solution.py:77
  127.3 216.8 %all-gather.7.cloned.1.call-start = ((), (), s32[]{:S(2)}) async-start(), calls=%async_computation.14 | async-start | bytes 10485760 | tf_op jit(solution)/shard_map/all_gather | solution.py:81
  278.8 97.5 %reduce-scatter.3.cloned.1.call-start = ((), (), s32[]{:S(2)}) async-start(), calls=%async_computation.15 | async-start | bytes 327680 | tf_op jit(solution)/shard_map/reduce_scatter | solution.py:84
  390.7 21.4 %all-to-all-start.4 = ((f32[32,48,128]{2,1,0:T(8,128)}), f32[32,48,128]{2,1,0:T(8,128)S(1)}, u32[]{:S(2)}, u32[]{:S(2)}) async-start(f32[32,48,128]{2,1,0:T(8,128)} %bitcast.26), calls=%async_computation.5 | async-start | bytes 1572864 | tf_op jit(solution)/shard_map/all_to_all | solution.py:55
  426.7 14.1 %all-to-all-start.5 = ((bf16[32,48,128]{2,1,0:T(8,128)(2,1)}), bf16[32,48,128]{2,1,0:T(8,128)(2,1)S(1)}, u32[]{:S(2)}, u32[]{:S(2)}) async-start(bf16[32,48,128]{2,1,0:T(8,128)(2,1)} %broadcast_select_fusion.2), calls=%async_computation.6 | async-start | bytes 786432 | tf_op jit(solution)/shard_map/all_to_all | solution.py:39
  432.3 14.3 %copy-start.2 = (bf16[4,768,128]{1,2,0:T(8,128)(2,1)S(1)}, bf16[4,768,128]{1,2,0:T(8,128)(2,1)}, u32[]{:S(2)}) copy-start(bf16[4,768,128]{1,2,0:T(8,128)(2,1)} %copy.78) | copy-start | bytes 2359300
  458.5 15.6 %all-to-all-start.6 = ((f32[32,48,128]{2,1,0:T(8,128)}), f32[32,48,128]{2,1,0:T(8,128)S(1)}, u32[]{:S(2)}, u32[]{:S(2)}) async-start(f32[32,48,128]{2,1,0:T(8,128)} %bitcast.138), calls=%async_computation.7 | async-start | bytes 1572864 | tf_op jit(solution)/shard_map/all_to_all | solution.py:55
  491.9 14.2 %all-to-all-start.7 = ((bf16[32,48,128]{2,1,0:T(8,128)(2,1)}), bf16[32,48,128]{2,1,0:T(8,128)(2,1)S(1)}, u32[]{:S(2)}, u32[]{:S(2)}) async-start(bf16[32,48,128]{2,1,0:T(8,128)(2,1)} %broadcast_select_fusion.1), calls=%async_computation.8 | async-start | bytes 786432 | tf_op jit(solution)/shard_map/all_to_all | solution.py:39
  496.4 166.4 %all-gather.9.cloned.1.call-start = ((), (), s32[]{:S(2)}) async-start(), calls=%async_computation.16 | async-start | bytes 2162688 | tf_op jit(solution)/shard_map/all_gather | solution.py:77
  513.0 215.1 %all-gather.11.cloned.1.call-start = ((), (), s32[]{:S(2)}) async-start(), calls=%async_computation.17 | async-start | bytes 10485760 | tf_op jit(solution)/shard_map/all_gather | solution.py:81
  662.9 97.4 %reduce-scatter.5.cloned.1.call-start = ((), (), s32[]{:S(2)}) async-start(), calls=%async_computation.18 | async-start | bytes 327680 | tf_op jit(solution)/shard_map/reduce_scatter | solution.py:84
  777.2 21.4 %all-to-all-start.8 = ((f32[32,48,128]{2,1,0:T(8,128)}), f32[32,48,128]{2,1,0:T(8,128)S(1)}, u32[]{:S(2)}, u32[]{:S(2)}) async-start(f32[32,48,128]{2,1,0:T(8,128)} %bitcast.139), calls=%async_computation.10 | async-start | bytes 1572864 | tf_op jit(solution)/shard_map/all_to_all | solution.py:55
  814.1 15.4 %copy-start.9 = (s32[1024]{0:T(1024)S(1)}, s32[1024]{0:T(1024)}, u32[]{:S(2)}) copy-start(s32[1024]{0:T(1024)} %copy-done.7) | copy-start | bytes 12292
  815.2 14.4 %all-to-all-start.9 = ((bf16[32,48,128]{2,1,0:T(8,128)(2,1)}), bf16[32,48,128]{2,1,0:T(8,128)(2,1)S(1)}, u32[]{:S(2)}, u32[]{:S(2)}) async-start(bf16[32,48,128]{2,1,0:T(8,128)(2,1)} %broadcast_select_fusion), calls=%async_computation.11 | async-start | bytes 786432 | tf_op jit(solution)/shard_map/all_to_all | solution.py:39
  845.4 15.6 %all-to-all-start.10 = ((f32[32,48,128]{2,1,0:T(8,128)}), f32[32,48,128]{2,1,0:T(8,128)S(1)}, u32[]{:S(2)}, u32[]{:S(2)}) async-start(f32[32,48,128]{2,1,0:T(8,128)} %bitcast.136), calls=%async_computation.12 | async-start | bytes 1572864 | tf_op jit(solution)/shard_map/all_to_all | solution.py:55
  (4 other events, 31.7 us)
Sparse Core Ops, SparseCore 0:
  127.4 151.3 all-gather.4
  280.4 63.5 all-gather.6
  349.9 26.2 reduce-scatter.2
  513.1 149.6 all-gather.8
  664.5 63.5 all-gather.10
  734.0 26.2 reduce-scatter.4
where the time goes:
time: 891 us; the launch traced here: 880 us
  waiting for transfers between devices  583 us (65%)
  local copies, waits for them, and re-layouts  93.7 us (11%)
  other arithmetic  83.6 us (9%)
  starting transfers between devices  57.9 us (6%)
  matrix products  47.3 us (5%)
  between operations  14.9 us (2%)
    all_gather x2, waiting for transfers between devices, shards(): gathered = lax.all_gather(solve_projection, 'wide', axis=0, tiled=True)  301 us
    all_gather x2, waiting for transfers between devices, shards(): lax.all_gather(gathered, 'narrow', axis=1, tiled=True)  130 us
    reduce_scatter x2, waiting for transfers between devices, shards(): lax.psum_scatter(partial_sums, 'narrow', scatter_dimension=1, tiled=True)  52.9 us
    scatter-add x5, other arithmetic, assemble_parts(): return summed.at[picked].add(incoming.reshape(owners * capacity, col_count))  50.2 us
    all_to_all x5, waiting for transfers between devices, assemble_parts(): lax.all_to_all(outgoing.reshape(owners, capacity, col_count), 'wide', spl...  46.7 us
    all_to_all x5, waiting for transfers between devices, gather_local(): lax.all_to_all(outgoing.reshape(owners, capacity, col_count), 'wide', spl...  45.1 us
    dot_general x5, matrix products, apply_each(): jnp.einsum('sij,sjc->sic', matrices, vectors, preferred_element_type=jnp....  31.6 us
    all_to_all x5, starting transfers between devices, assemble_parts(): lax.all_to_all(outgoing.reshape(owners, capacity, col_count), 'wide', spl...  26.4 us
  transfers between devices with their start and end apart: 17, of which 17 were waited for; matrix products, arithmetic and copies ran while one was open for 2% of the time, Pallas kernels for 0%

commit v1 on v0

--- a/solution.py
+++ b/solution.py
@@ -1,3 +1,4 @@
+import functools
 import jax
 import jax.numpy as jnp
 from jax import lax
@@ -5,6 +6,16 @@
 
 ITERS = 2
 damping = 0.5
+
+
+def _place_targets(arr, ax_name, ndim_at):
+    kept_arr = lax.axis_size(ax_name)
+    part_next = jnp.stack(kept_arr * [arr])
+    passed = lax.all_to_all(part_next, ax_name, 0, 0)
+    return jnp.concatenate(passed, ndim_at)
+
+
+search_the_indices = functools.partial(_place_targets, ax_name="narrow", ndim_at=1)
 
 
 def apply_each(matrices, vectors):
@@ -77,9 +88,7 @@
         gathered = lax.all_gather(solve_projection, "wide", axis=0, tiled=True)
         tile_width = coarse_inverse.shape[1]
         row_offset = lax.axis_index("narrow") * tile_width
-        selected = lax.dynamic_slice_in_dim(
-            lax.all_gather(gathered, "narrow", axis=1, tiled=True), row_offset, tile_width, 0
-        )
+        selected = lax.dynamic_slice_in_dim(search_the_indices(gathered), row_offset, tile_width, 0)
         partial_sums = jnp.dot(coarse_inverse, selected, precision=lax.Precision.HIGHEST)
         coarse = lax.psum_scatter(partial_sums, "narrow", scatter_dimension=1, tiled=True)
         lifted = jnp.einsum(

time: 891 us -> 965 us (1.083)
  blocking collectives: 0 us -> 98.9 us
  waiting for transfers between devices: 583 us -> 546 us
  local copies, waits for them, and re-layouts: 93.7 us -> 106 us
    all_gather x2 -> x0, waiting for transfers between devices: 130 us -> none  [shards(): lax.all_gather(gathered, 'narrow', axis=1, tiled=True)]
    all_to_all x0 -> x1, blocking collectives: none -> 98.9 us  [_place_targets(): passed = lax.all_to_all(part_next, ax_name, 0, 0)]
    all_to_all x0 -> x1, waiting for transfers between devices: none -> 94.6 us  [_place_targets(): passed = lax.all_to_all(part_next, ax_name, 0, 0)]
  transfers between devices with their start and end apart: 17 -> 16, of which waited for: 17 -> 16; matrix products, arithmetic and copies ran while one was open for 2% -> 2% of each run, Pallas kernels for 0% -> 0%
where the time goes in v1:
time: 965 us; the launch traced here: 954 us
  waiting for transfers between devices  546 us (57%)
  local copies, waits for them, and re-layouts  106 us (11%)
  blocking collectives  98.9 us (10%)
  other arithmetic  83.4 us (9%)
  starting transfers between devices  63.3 us (7%)
  matrix products  42.5 us (4%)
  between operations  14.6 us (2%)
    all_gather x2, waiting for transfers between devices, shards(): gathered = lax.all_gather(solve_projection, 'wide', axis=0, tiled=True)  301 us
    all_to_all x1, blocking collectives, _place_targets(): passed = lax.all_to_all(part_next, ax_name, 0, 0)  98.9 us
    all_to_all x1, waiting for transfers between devices, _place_targets(): passed = lax.all_to_all(part_next, ax_name, 0, 0)  94.6 us
    reduce_scatter x2, waiting for transfers between devices, shards(): lax.psum_scatter(partial_sums, 'narrow', scatter_dimension=1, tiled=True)  51.1 us
    scatter-add x5, other arithmetic, assemble_parts(): return summed.at[picked].add(incoming.reshape(owners * capacity, col_count))  50 us
    all_to_all x5, waiting for transfers between devices, assemble_parts(): lax.all_to_all(outgoing.reshape(owners, capacity, col_count), 'wide', spl...  46.7 us
    all_to_all x5, waiting for transfers between devices, gather_local(): lax.all_to_all(outgoing.reshape(owners, capacity, col_count), 'wide', spl...  45 us
    dot_general x5, matrix products, apply_each(): jnp.einsum('sij,sjc->sic', matrices, vectors, preferred_element_type=jnp....  31.6 us
  transfers between devices with their start and end apart: 16, of which 16 were waited for; matrix products, arithmetic and copies ran while one was open for 2% of the time, Pallas kernels for 0%

profile of v1, /device:TPU:0, one launch (start us, length us, event | category | flops | bytes accessed | tf_op | source)
XLA Modules:
  0.0 953.9 jit_solution(1060679815799019603)
XLA Ops:
  10.8 9.0 reduce-window.6
  25.4 8.8 all-to-all-start
  52.2 9.4 all-to-all-done.1
  84.6 8.8 all-to-all-done.2
  93.4 9.5 scatter_fusion
  113.6 9.2 all-to-all-done.3
  127.3 151.5 %all-gather.3.cloned.1.call-done = f32[4096,128]{1,0:T(8,128)} async-done(((f32[128,128]{1,0:T(8,128)}), f32[4096,128]{1,0:T(8,128)}) %all-gather.3.cloned.1.call-update) | async-done | bytes 2097168 | tf_op jit(solution)/shard_map/all_gather | solution.py:88
  290.8 94.6 %all-to-all-done.4 = f32[4,4096,128]{1,2,0:T(8,128)} async-done(((f32[4,4096,128]{1,2,0:T(8,128)}), f32[4,4096,128]{1,2,0:T(8,128)}, u32[]{:S(2)}, u32[]{:S(2)}) %all-to-all-start.4) | async-done | bytes 8388640 | tf_op jit(solution)/shard_map/all_to_all | solution.py:14
  389.6 25.8 %reduce-scatter.3.cloned.1.call-done = f32[128,128]{0,1:T(8,128)} async-done(((f32[128,512]{0,1:T(8,128)}), f32[128,128]{0,1:T(8,128)}) %reduce-scatter.3.cloned.1.call-update) | async-done | bytes 65552 | tf_op jit(solution)/shard_map/reduce_scatter | solution.py:93
  429.8 7.2 all-to-all-start.5
  439.1 12.1 %all-to-all-done.5 = f32[32,48,128]{2,1,0:T(8,128)S(1)} async-done(((f32[32,48,128]{2,1,0:T(8,128)}), f32[32,48,128]{2,1,0:T(8,128)S(1)}, u32[]{:S(2)}, u32[]{:S(2)}) %all-to-all-start.5) | async-done | bytes 786464 | tf_op jit(solution)/shard_map/all_to_all | solution.py:66
  451.2 9.5 scatter_fusion.1
  471.4 8.5 all-to-all-done.6
  513.3 10.8 %scatter_fusion.2 = f32[3072,128]{1,0:T(8,128)} fusion(f32[3072,128]{1,0:T(8,128)} %bitcast.126, s32[1536]{0:T(1024)S(1)} %fusion.35, f32[1536,128]{1,0:T(8,128)S(1)} %bitcast.140), kind=kCustom, calls=%fused_computation.16 | custom fusion | flops 196608 | bytes 2365440 | tf_op jit(solution)/shard_map/scatter-add | solution.py:74
  536.8 8.5 all-to-all-done.8
  552.2 149.8 %all-gather.5.cloned.1.call-done = f32[4096,128]{1,0:T(8,128)} async-done(((f32[128,128]{1,0:T(8,128)}), f32[4096,128]{1,0:T(8,128)}) %all-gather.5.cloned.1.call-update) | async-done | bytes 2097168 | tf_op jit(solution)/shard_map/all_gather | solution.py:88
  707.6 98.9 %all_to_all.72 = f32[4,4096,128]{1,2,0:T(8,128)S(1)} all-to-all(f32[4,4096,128]{1,2,0:T(8,128)S(1)} %stack.5), channel_id=1, replica_groups=mesh['wide'=32,'narrow'=4] {'narrow'}, dimensions={0} | all-to-all | bytes 16777216 | tf_op jit(solution)/shard_map/all_to_all | solution.py:14
  809.0 25.3 %reduce-scatter.5.cloned.1.call-done = f32[128,128]{0,1:T(8,128)} async-done(((f32[128,512]{0,1:T(8,128)}), f32[128,128]{0,1:T(8,128)}) %reduce-scatter.5.cloned.1.call-update) | async-done | bytes 65552 | tf_op jit(solution)/shard_map/reduce_scatter | solution.py:93
  851.3 7.2 all-to-all-start.10
  861.2 11.5 %all-to-all-done.10 = f32[32,48,128]{2,1,0:T(8,128)S(1)} async-done(((f32[32,48,128]{2,1,0:T(8,128)}), f32[32,48,128]{2,1,0:T(8,128)S(1)}, u32[]{:S(2)}, u32[]{:S(2)}) %all-to-all-start.10) | async-done | bytes 786464 | tf_op jit(solution)/shard_map/all_to_all | solution.py:66
  872.6 10.8 %scatter_fusion.3 = f32[3072,128]{1,0:T(8,128)} fusion(f32[3072,128]{1,0:T(8,128)} %bitcast_add_fusion, s32[1536]{0:T(1024)S(1)} %fusion.35, f32[1536,128]{1,0:T(8,128)S(1)} %bitcast.141), kind=kCustom, calls=%fused_computation.18 | custom fusion | flops 196608 | bytes 2365440 | tf_op jit(solution)/shard_map/scatter-add | solution.py:74
  894.1 9.4 all-to-all-done.11
  926.6 8.5 all-to-all-done.12
  935.0 9.5 scatter_fusion.4
  (149 shorter events, 225.3 us)
Async XLA Ops:
  7.2 378.3 %copy-start = (f32[128,1024]{1,0:T(8,128)S(1)}, f32[128,1024]{1,0:T(8,128)}, u32[]{:S(2)}) copy-start(f32[128,1024]{1,0:T(8,128)} %param.12) | copy-start | bytes 1572868
  20.3 52.7 %copy-start.12 = (s32[1024,1]{0,1:T(1,128)}, s32[1024,1]{0,1:T(1,128)S(1)}, u32[]{:S(2)}) copy-start(s32[1024,1]{0,1:T(1,128)S(1)} %compare_select_fusion.2) | copy-start | bytes 12292
  25.4 17.0 %all-to-all-start = ((s32[32,1,48]{2,1,0:T(1,128)}), s32[32,1,48]{2,1,0:T(1,128)S(1)}, u32[]{:S(2)}, u32[]{:S(2)}) async-start(s32[32,1,48]{2,1,0:T(1,128)} %all_to_all.44), calls=%async_computation | async-start | bytes 32768 | tf_op jit(solution)/shard_map/all_to_all | solution.py:41
  42.4 65.3 %copy-start.7 = (pred[32,48]{1,0:T(8,128)(4,1)}, pred[32,48]{1,0:T(8,128)(4,1)S(1)}, u32[]{:S(2)}) copy-start(pred[32,48]{1,0:T(8,128)(4,1)S(1)} %compare_bitcast_fusion) | copy-start | bytes 4612
  48.0 13.6 %all-to-all-start.1 = ((bf16[32,48,128]{2,1,0:T(8,128)(2,1)}), bf16[32,48,128]{2,1,0:T(8,128)(2,1)S(1)}, u32[]{:S(2)}, u32[]{:S(2)}) async-start(bf16[32,48,128]{2,1,0:T(8,128)(2,1)} %broadcast_select_fusion.4), calls=%async_computation.1 | async-start | bytes 786432 | tf_op jit(solution)/shard_map/all_to_all | solution.py:50
  52.1 19.8 %copy-start.9 = (s32[1024]{0:T(1024)}, s32[1024]{0:T(1024)S(1)}, u32[]{:S(2)}) copy-start(s32[1024]{0:T(1024)S(1)} %broadcast_clamp_fusion) | copy-start | bytes 12292
  77.4 16.0 %all-to-all-start.2 = ((f32[32,48,128]{2,1,0:T(8,128)}), f32[32,48,128]{2,1,0:T(8,128)S(1)}, u32[]{:S(2)}, u32[]{:S(2)}) async-start(f32[32,48,128]{2,1,0:T(8,128)} %bitcast.144), calls=%async_computation.2 | async-start | bytes 1572864 | tf_op jit(solution)/shard_map/all_to_all | solution.py:66
  107.6 15.2 %copy-start.10 = (s32[1024]{0:T(1024)S(1)}, s32[1024]{0:T(1024)}, u32[]{:S(2)}) copy-start(s32[1024]{0:T(1024)} %copy-done.9) | copy-start | bytes 12292
  108.7 14.1 %all-to-all-start.3 = ((bf16[32,48,128]{2,1,0:T(8,128)(2,1)}), bf16[32,48,128]{2,1,0:T(8,128)(2,1)S(1)}, u32[]{:S(2)}, u32[]{:S(2)}) async-start(bf16[32,48,128]{2,1,0:T(8,128)(2,1)} %broadcast_select_fusion.3), calls=%async_computation.3 | async-start | bytes 786432 | tf_op jit(solution)/shard_map/all_to_all | solution.py:50
  113.1 165.7 %all-gather.3.cloned.1.call-start = ((), (), s32[]{:S(2)}) async-start(), calls=%async_computation.15 | async-start | bytes 2162688 | tf_op jit(solution)/shard_map/all_gather | solution.py:88
  285.1 100.3 %all-to-all-start.4 = ((f32[4,4096,128]{1,2,0:T(8,128)}), f32[4,4096,128]{1,2,0:T(8,128)}, u32[]{:S(2)}, u32[]{:S(2)}) async-start(f32[4,4096,128]{1,2,0:T(8,128)} %stack.4), calls=%async_computation.4 | async-start | bytes 16777216 | tf_op jit(solution)/shard_map/all_to_all | solution.py:14
  290.8 124.6 %reduce-scatter.3.cloned.1.call-start = ((), (), s32[]{:S(2)}) async-start(), calls=%async_computation.16 | async-start | bytes 327680 | tf_op jit(solution)/shard_map/reduce_scatter | solution.py:93
  389.6 27.9 %copy-start.4 = (bf16[4,768,128]{1,2,0:T(8,128)(2,1)S(1)}, bf16[4,768,128]{1,2,0:T(8,128)(2,1)}, u32[]{:S(2)}) copy-start(bf16[4,768,128]{1,2,0:T(8,128)(2,1)} %copy-done.3) | copy-start | bytes 2359300
  429.8 21.4 %all-to-all-start.5 = ((f32[32,48,128]{2,1,0:T(8,128)}), f32[32,48,128]{2,1,0:T(8,128)S(1)}, u32[]{:S(2)}, u32[]{:S(2)}) async-start(f32[32,48,128]{2,1,0:T(8,128)} %bitcast.28), calls=%async_computation.6 | async-start | bytes 1572864 | tf_op jit(solution)/shard_map/all_to_all | solution.py:66
  465.6 14.3 %all-to-all-start.6 = ((bf16[32,48,128]{2,1,0:T(8,128)(2,1)}), bf16[32,48,128]{2,1,0:T(8,128)(2,1)S(1)}, u32[]{:S(2)}, u32[]{:S(2)}) async-start(bf16[32,48,128]{2,1,0:T(8,128)(2,1)} %broadcast_select_fusion.2), calls=%async_computation.7 | async-start | bytes 786432 | tf_op jit(solution)/shard_map/all_to_all | solution.py:50
  471.4 14.3 %copy-start.2 = (bf16[4,768,128]{1,2,0:T(8,128)(2,1)S(1)}, bf16[4,768,128]{1,2,0:T(8,128)(2,1)}, u32[]{:S(2)}) copy-start(bf16[4,768,128]{1,2,0:T(8,128)(2,1)} %copy.83) | copy-start | bytes 2359300
  497.7 15.6 %all-to-all-start.7 = ((f32[32,48,128]{2,1,0:T(8,128)}), f32[32,48,128]{2,1,0:T(8,128)S(1)}, u32[]{:S(2)}, u32[]{:S(2)}) async-start(f32[32,48,128]{2,1,0:T(8,128)} %bitcast.145), calls=%async_computation.8 | async-start | bytes 1572864 | tf_op jit(solution)/shard_map/all_to_all | solution.py:66
  531.1 14.2 %all-to-all-start.8 = ((bf16[32,48,128]{2,1,0:T(8,128)(2,1)}), bf16[32,48,128]{2,1,0:T(8,128)(2,1)S(1)}, u32[]{:S(2)}, u32[]{:S(2)}) async-start(bf16[32,48,128]{2,1,0:T(8,128)(2,1)} %broadcast_select_fusion.1), calls=%async_computation.9 | async-start | bytes 786432 | tf_op jit(solution)/shard_map/all_to_all | solution.py:50
  535.6 166.4 %all-gather.5.cloned.1.call-start = ((), (), s32[]{:S(2)}) async-start(), calls=%async_computation.17 | async-start | bytes 2162688 | tf_op jit(solution)/shard_map/all_gather | solution.py:88
  552.2 282.1 %reduce-scatter.5.cloned.1.call-start = ((), (), s32[]{:S(2)}) async-start(), calls=%async_computation.18 | async-start | bytes 327680 | tf_op jit(solution)/shard_map/reduce_scatter | solution.py:93
  851.3 21.4 %all-to-all-start.10 = ((f32[32,48,128]{2,1,0:T(8,128)}), f32[32,48,128]{2,1,0:T(8,128)S(1)}, u32[]{:S(2)}, u32[]{:S(2)}) async-start(f32[32,48,128]{2,1,0:T(8,128)} %bitcast.146), calls=%async_computation.12 | async-start | bytes 1572864 | tf_op jit(solution)/shard_map/all_to_all | solution.py:66
  888.1 15.4 %copy-start.11 = (s32[1024]{0:T(1024)S(1)}, s32[1024]{0:T(1024)}, u32[]{:S(2)}) copy-start(s32[1024]{0:T(1024)} %copy-done.9) | copy-start | bytes 12292
  889.2 14.4 %all-to-all-start.11 = ((bf16[32,48,128]{2,1,0:T(8,128)(2,1)}), bf16[32,48,128]{2,1,0:T(8,128)(2,1)S(1)}, u32[]{:S(2)}, u32[]{:S(2)}) async-start(bf16[32,48,128]{2,1,0:T(8,128)(2,1)} %broadcast_select_fusion), calls=%async_computation.13 | async-start | bytes 786432 | tf_op jit(solution)/shard_map/all_to_all | solution.py:50
  919.4 15.6 %all-to-all-start.12 = ((f32[32,48,128]{2,1,0:T(8,128)}), f32[32,48,128]{2,1,0:T(8,128)S(1)}, u32[]{:S(2)}, u32[]{:S(2)}) async-start(f32[32,48,128]{2,1,0:T(8,128)} %bitcast.143), calls=%async_computation.14 | async-start | bytes 1572864 | tf_op jit(solution)/shard_map/all_to_all | solution.py:66
  (5 other events, 45.3 us)
Sparse Core Ops, SparseCore 0:
  127.4 151.3 all-gather.2
  389.7 25.6 reduce-scatter.2
  552.3 149.7 all-gather.4
  809.2 25.0 reduce-scatter.4
